TPU v7x, 512 devices: a whole 4x8x8 slice. The times are simulated.
512 devices in a mesh: dp: 2 (over core), ctx: 64 (over z, y), head: 4 (over x).
Axes of the slice: x: 4, y: 8, z: 8, core: 2. Of those that a mesh axis runs over, the one named last changes fastest.
Arguments:
- queries: bfloat16 [2, 8192, 2560], P('dp', 'ctx', 'head'), may hold values from -25 to 25
- keys: bfloat16 [2, 8192, 2560], P('dp', 'ctx', 'head'), may hold values from -25 to 25
- values: bfloat16 [2, 8192, 2560], P('dp', 'ctx', 'head'), may hold values from -6 to 6
- grad_y: bfloat16 [2, 8192, 2560], P('dp', 'ctx', 'head'), may hold values from -6 to 6
- out_gain: float32 [2560], P('head'), may hold values from 0.1 to 1.9
- offsets: int32 [2, 20], P(None, 'head'), may hold values from 0 to 63, as said below
Outputs:
- attended: bfloat16 [2, 8192, 2560], P('dp', 'ctx', 'head')
- query_grad: bfloat16 [2, 8192, 2560], P('dp', 'ctx', 'head')
- key_grad: bfloat16 [2, 8192, 2560], P('dp', 'ctx', 'head')
- value_grad: bfloat16 [2, 8192, 2560], P('dp', 'ctx', 'head')
- gain_grad: float32 [2560], P('head')
Inputs may be any that keep to these rules, and one draw needn't show every extreme that they name: Row 0 holds offsets below 8, row 1 offsets below 64.
All inputs are finite; a program needn't handle non-finite values.
Results may differ from a plain program's by a relative error of at most 0.011.
Values may be sent and summed in bfloat16 or wider, within the bound.
A program may use at most 64 MiB of HBM per device.

v0:
```python
import math
import jax
import jax.numpy as jnp
from jax import lax
from jax.sharding import PartitionSpec as P

HEAD_DIM = 128
SPAN = 4
R1 = 8
EPS = 1e-06


def group_gather(block, axis, group):
    count = lax.axis_size(axis)
    pieces = [block]
    for shift in range(1, group):
        route = []
        for src in range(count):
            base = src - src % group
            route.append((src, base + (src % group + shift) % group))
        pieces.append(lax.ppermute(block, axis, route))
    return jnp.concatenate(pieces, 0)


def pick_rows(source_rows, dilation, shifts):
    row_count, head_count, head_width = source_rows.shape
    grouped = source_rows.reshape(row_count // dilation, dilation, head_count, head_width)
    hit_mask = jnp.arange(dilation, dtype=jnp.int32).reshape(1, dilation, 1, 1) == shifts.reshape(
        1, 1, head_count, 1
    )
    chosen = jnp.where(hit_mask, grouped, jnp.zeros((), source_rows.dtype))
    return jnp.sum(chosen, axis=1, dtype=source_rows.dtype)


def place_rows(row_values, dilation, shifts):
    row_count, head_count, head_width = row_values.shape
    hit_mask = jnp.arange(dilation, dtype=jnp.int32).reshape(1, dilation, 1, 1) == shifts.reshape(
        1, 1, head_count, 1
    )
    spread = jnp.where(hit_mask, row_values[:, None], jnp.zeros((), row_values.dtype))
    return spread.reshape(row_count * dilation, head_count, head_width)


def level_scores(q_rows, k_rows):
    score_scale = 1.0 / math.sqrt(q_rows.shape[-1])
    return (
        jnp.einsum("qhe,khe->hqk", q_rows, k_rows, preferred_element_type=jnp.float32) * score_scale
    )


def attend(q_rows, k_rows, v_rows):
    scores = level_scores(q_rows, k_rows)
    row_max = jnp.max(scores, axis=-1, keepdims=True)
    log_total = row_max[..., 0] + jnp.log(jnp.sum(jnp.exp(scores - row_max), axis=-1))
    soft_rows = jnp.exp(scores - log_total[..., None]).astype(jnp.bfloat16)
    level_out = jnp.einsum("hqk,khe->qhe", soft_rows, v_rows, preferred_element_type=jnp.float32)
    return (level_out, log_total.T)


def score_grads(q_rows, k_rows, v_rows, log_total, grad_low, row_shift):
    score_scale = 1.0 / math.sqrt(q_rows.shape[-1])
    scores = level_scores(q_rows, k_rows)
    exact_soft = jnp.exp(scores - log_total.T[..., None])
    prob_grad = jnp.einsum("qhe,khe->hqk", grad_low, v_rows, preferred_element_type=jnp.float32)
    score_grad = (exact_soft * (prob_grad + row_shift.T[..., None]) * score_scale).astype(
        jnp.bfloat16
    )
    return (score_grad, exact_soft.astype(jnp.bfloat16))


def key_parts(score_grad, soft_low, q_rows, grad_low):
    k_part = jnp.einsum("hqk,qhe->khe", score_grad, q_rows, preferred_element_type=jnp.float32)
    v_part = jnp.einsum("hqk,qhe->khe", soft_low, grad_low, preferred_element_type=jnp.float32)
    return (k_part, v_part)


def query_part(score_grad, k_rows):
    return jnp.einsum("hqk,khe->qhe", score_grad, k_rows, preferred_element_type=jnp.float32)


def split_qkv(packed, head_count):
    width = head_count * HEAD_DIM
    shape = (packed.shape[0], head_count, HEAD_DIM)
    return tuple((packed[:, i * width : (i + 1) * width].reshape(shape) for i in range(3)))


def pack_grads(grad_low, row_shift):
    rows = grad_low.shape[0]
    return jnp.concatenate(
        [grad_low.astype(jnp.float32).reshape(rows, -1), row_shift.astype(jnp.float32)], 1
    )


def unpack_grads(packed, head_count):
    width = head_count * HEAD_DIM
    grad_low = packed[:, :width].astype(jnp.bfloat16).reshape(-1, head_count, HEAD_DIM)
    return (grad_low, packed[:, width:])


def shards(queries, keys, values, grad_y, out_gain, offsets):
    tokens = queries.shape[1]
    flat_width = queries.shape[2]
    head_count = flat_width // HEAD_DIM
    row_shape = (tokens, head_count, HEAD_DIM)
    q_own = queries[0].reshape(row_shape)
    k_own = keys[0].reshape(row_shape)
    v_own = values[0].reshape(row_shape)
    ctx_size = lax.axis_size("ctx")
    my_place = lax.axis_index("ctx")
    mid_shift = offsets[0]
    top_shift = offsets[1]
    positions = jnp.arange(tokens, dtype=jnp.int32)
    mid_hit = (positions % R1)[:, None] == mid_shift[None, :]
    top_hit = (positions % ctx_size)[:, None] == top_shift[None, :]
    mid_pack = jnp.concatenate(
        [pick_rows(x, R1, mid_shift).reshape(-1, flat_width) for x in (q_own, k_own, v_own)], 1
    )
    top_pack = jnp.concatenate(
        [pick_rows(x, ctx_size, top_shift).reshape(-1, flat_width) for x in (q_own, k_own, v_own)],
        1,
    )
    mid_rows = mid_pack.shape[0]
    top_rows = top_pack.shape[0]
    mid_all = group_gather(mid_pack, "ctx", SPAN)
    top_all = lax.all_gather(top_pack, "ctx", axis=0, tiled=True)
    mid_q, mid_k, mid_v = split_qkv(mid_all, head_count)
    top_q, top_k, top_v = split_qkv(top_all, head_count)
    top_start = my_place * top_rows
    base_out, base_total = attend(q_own, k_own, v_own)
    mid_out_all, mid_total_all = attend(mid_q, mid_k, mid_v)
    top_out_all, top_total_all = attend(top_q, top_k, top_v)
    mid_out = mid_out_all[:mid_rows]
    mid_total = mid_total_all[:mid_rows]
    top_out = lax.dynamic_slice_in_dim(top_out_all, top_start, top_rows, 0)
    top_total = lax.dynamic_slice_in_dim(top_total_all, top_start, top_rows, 0)
    mid_full = place_rows(mid_total[..., None], R1, mid_shift)[..., 0]
    top_full = place_rows(top_total[..., None], ctx_size, top_shift)[..., 0]
    row_max = jnp.maximum(base_total, jnp.where(mid_hit, mid_full, base_total))
    row_max = jnp.maximum(row_max, jnp.where(top_hit, top_full, base_total))
    base_expo = jnp.exp(base_total - row_max)
    mid_expo = jnp.where(mid_hit, jnp.exp(mid_full - row_max), 0.0)
    top_expo = jnp.where(top_hit, jnp.exp(top_full - row_max), 0.0)
    denom = base_expo + mid_expo + top_expo
    base_share = base_expo / denom
    mid_share = mid_expo / denom
    top_share = top_expo / denom
    attn = (
        base_share[..., None] * base_out
        + mid_share[..., None] * place_rows(mid_out, R1, mid_shift)
        + top_share[..., None] * place_rows(top_out, ctx_size, top_shift)
    )
    inv_rms = lax.rsqrt(jnp.mean(attn * attn, axis=-1, keepdims=True) + EPS)
    normed = attn * inv_rms
    gain_rows = out_gain.reshape(head_count, HEAD_DIM)
    attended = (normed * gain_rows).astype(jnp.bfloat16).reshape(1, tokens, flat_width)
    grad_full = grad_y[0].reshape(row_shape).astype(jnp.float32)
    gain_part = jnp.sum(grad_full * normed, axis=0).reshape(flat_width)
    grad_norm = grad_full * gain_rows
    grad_attn = inv_rms * (
        grad_norm - normed * jnp.mean(grad_norm * normed, axis=-1, keepdims=True)
    )
    inner = jnp.sum(grad_attn * attn, axis=-1)
    base_low = (base_share[..., None] * grad_attn).astype(jnp.bfloat16)
    base_shift = -(base_share * inner)
    base_grad, base_soft = score_grads(q_own, k_own, v_own, base_total, base_low, base_shift)
    base_dq = query_part(base_grad, k_own)
    base_dk, base_dv = key_parts(base_grad, base_soft, q_own, base_low)
    mid_sel = pick_rows(mid_share[..., None], R1, mid_shift)[..., 0]
    mid_low = (mid_sel[..., None] * pick_rows(grad_attn, R1, mid_shift)).astype(jnp.bfloat16)
    mid_row_shift = -(mid_sel * pick_rows(inner[..., None], R1, mid_shift)[..., 0])
    top_sel = pick_rows(top_share[..., None], ctx_size, top_shift)[..., 0]
    top_low = (top_sel[..., None] * pick_rows(grad_attn, ctx_size, top_shift)).astype(jnp.bfloat16)
    top_row_shift = -(top_sel * pick_rows(inner[..., None], ctx_size, top_shift)[..., 0])
    mid_low_all, mid_shift_all = unpack_grads(
        group_gather(pack_grads(mid_low, mid_row_shift), "ctx", SPAN), head_count
    )
    top_grads = pack_grads(top_low, top_row_shift)
    gain_row = jnp.pad(gain_part, (0, top_grads.shape[1] - flat_width))[None]
    gathered = lax.all_gather(jnp.concatenate([top_grads, gain_row], 0), "ctx", axis=0)
    top_low_all, top_shift_all = unpack_grads(
        gathered[:, :top_rows].reshape(-1, top_grads.shape[1]), head_count
    )
    gain_grad = lax.psum(jnp.sum(gathered[:, top_rows, :flat_width], axis=0), "dp")
    mid_grad, mid_soft = score_grads(mid_q, mid_k, mid_v, mid_total_all, mid_low_all, mid_shift_all)
    mid_dq = query_part(mid_grad[:, :mid_rows], mid_k)
    mid_dk, mid_dv = key_parts(
        mid_grad[:, :, :mid_rows], mid_soft[:, :, :mid_rows], mid_q, mid_low_all
    )
    top_grad, top_soft = score_grads(top_q, top_k, top_v, top_total_all, top_low_all, top_shift_all)
    own_grad = lax.dynamic_slice_in_dim(top_grad, top_start, top_rows, 1)
    top_dq = query_part(own_grad, top_k)
    key_grad_cols = lax.dynamic_slice_in_dim(top_grad, top_start, top_rows, 2)
    key_soft_cols = lax.dynamic_slice_in_dim(top_soft, top_start, top_rows, 2)
    top_dk, top_dv = key_parts(key_grad_cols, key_soft_cols, top_q, top_low_all)
    query_grad = (
        base_dq + place_rows(mid_dq, R1, mid_shift) + place_rows(top_dq, ctx_size, top_shift)
    )
    key_grad = base_dk + place_rows(mid_dk, R1, mid_shift) + place_rows(top_dk, ctx_size, top_shift)
    value_grad = (
        base_dv + place_rows(mid_dv, R1, mid_shift) + place_rows(top_dv, ctx_size, top_shift)
    )
    out_shape = (1, tokens, flat_width)
    return (
        attended,
        query_grad.astype(jnp.bfloat16).reshape(out_shape),
        key_grad.astype(jnp.bfloat16).reshape(out_shape),
        value_grad.astype(jnp.bfloat16).reshape(out_shape),
        gain_grad,
    )


def solution(mesh):
    in_specs = (
        P("dp", "ctx", "head"),
        P("dp", "ctx", "head"),
        P("dp", "ctx", "head"),
        P("dp", "ctx", "head"),
        P("head"),
        P(None, "head"),
    )
    out_specs = (
        P("dp", "ctx", "head"),
        P("dp", "ctx", "head"),
        P("dp", "ctx", "head"),
        P("dp", "ctx", "head"),
        P("head"),
    )
    return jax.shard_map(shards, mesh=mesh, in_specs=in_specs, out_specs=out_specs, check_vma=False)
```

profile of v0, /device:TPU:1, one launch (start us, length us, event | category | flops | bytes accessed | tf_op | source)
XLA Modules:
  0.0 159.5 jit_solution(9887099655481750333)
XLA Ops:
  0.6 0.8 slice_bitcast_fusion.5
  1.5 1.5 fusion.24
  3.0 6.1 %collective-permute-start.2 = (bf16[16,1920]{1,0:T(8,128)(2,1)S(1)}, bf16[16,1920]{1,0:T(8,128)(2,1)S(1)}, u32[]{:S(2)}, u32[]{:S(2)}) collective-permute-start(bf16[16,1920]{1,0:T(8,128)(2,1)S(1)} %bitcast_dynamic-update-slice_fusion), channel_id=1, source_target_pairs={{0,12},{4,0},{8,4},{12,8},{16,28},{20,16},{24,20},{28,24},{32,44},... | collective-permute-start | bytes 184328 | tf_op jit(solution)/shard_map/ppermute | solution.py:21
  9.1 1.9 %collective-permute-start.1 = (bf16[16,1920]{1,0:T(8,128)(2,1)S(1)}, bf16[16,1920]{1,0:T(8,128)(2,1)S(1)}, u32[]{:S(2)}, u32[]{:S(2)}) collective-permute-start(bf16[16,1920]{1,0:T(8,128)(2,1)S(1)} %bitcast_dynamic-update-slice_fusion), channel_id=1, source_target_pairs={{0,8},{4,12},{8,0},{12,4},{16,24},{20,28},{24,16},{28,20},{32,40},... | collective-permute-start | bytes 184328 | tf_op jit(solution)/shard_map/ppermute | solution.py:21
  11.0 2.3 %collective-permute-start = (bf16[16,1920]{1,0:T(8,128)(2,1)S(1)}, bf16[16,1920]{1,0:T(8,128)(2,1)S(1)}, u32[]{:S(2)}, u32[]{:S(2)}) collective-permute-start(bf16[16,1920]{1,0:T(8,128)(2,1)S(1)} %bitcast_dynamic-update-slice_fusion), channel_id=1, source_target_pairs={{0,4},{4,8},{8,12},{12,0},{16,20},{20,24},{24,28},{28,16},{32,36},... | collective-permute-start | bytes 184328 | tf_op jit(solution)/shard_map/ppermute | solution.py:21
  13.4 0.2 copy.294
  13.6 0.7 copy-done.1
  14.5 0.7 copy-done.2
  15.4 0.2 reshape_reshape_squeeze.21
  15.6 0.2 reshape_reshape_squeeze.22
  15.8 0.2 reshape_reshape_squeeze.23
  16.4 0.3 copy-done.8
  17.0 0.3 select_reduce_fusion.2
  17.4 44.2 %all-gather.1 = bf16[64,2,1920]{2,1,0:T(2,128)(2,1)S(1)} all-gather(bf16[1,2,1920]{2,1,0:T(2,128)(2,1)S(1)} %maximum_bitcast_fusion.2), channel_id=1, replica_groups=mesh['dp'=2,'ctx'=64,'head'=4] {'ctx'}, dimensions={0}, use_global_device_ids=true | all-gather | bytes 499200 | tf_op jit(solution)/shard_map/all_gather | solution.py:125
  61.5 0.2 reshape.375
  61.8 0.2 copy.308
  62.0 0.2 copy.316
  62.1 0.2 copy.307
  62.3 0.3 fusion.67
  63.0 0.3 fusion.70
  63.4 0.3 fusion.69
  63.8 0.2 fusion.68
  64.5 0.2 convolution_bitcast_fusion.4
  65.0 0.2 fusion.20
  65.3 0.5 multiply_reduce_fusion.3
  65.8 0.7 copy-done.9
  66.5 0.8 multiply_reduce_fusion.2
  67.3 0.3 fusion.19
  67.6 0.2 multiply_reduce_fusion.1
  68.2 0.6 pad_maximum_fusion.2
  68.9 3.9 %collective-permute-start.5 = (f32[16,645]{1,0:T(8,128)}, f32[16,645]{1,0:T(8,128)}, u32[]{:S(2)}, u32[]{:S(2)}) collective-permute-start(f32[16,645]{1,0:T(8,128)} %pad_maximum_fusion.2), channel_id=1, source_target_pairs={{0,12},{4,0},{8,4},{12,8},{16,28},{20,16},{24,20},{28,24},{32,44},... | collective-permute-start | bytes 123848 | tf_op jit(solution)/shard_map/ppermute | solution.py:21
  72.8 2.8 %collective-permute-start.4 = (f32[16,645]{1,0:T(8,128)}, f32[16,645]{1,0:T(8,128)}, u32[]{:S(2)}, u32[]{:S(2)}) collective-permute-start(f32[16,645]{1,0:T(8,128)} %pad_maximum_fusion.2), channel_id=1, source_target_pairs={{0,8},{4,12},{8,0},{12,4},{16,24},{20,28},{24,16},{28,20},{32,40},... | collective-permute-start | bytes 123848 | tf_op jit(solution)/shard_map/ppermute | solution.py:21
  75.6 1.9 %collective-permute-start.3 = (f32[16,645]{1,0:T(8,128)}, f32[16,645]{1,0:T(8,128)}, u32[]{:S(2)}, u32[]{:S(2)}) collective-permute-start(f32[16,645]{1,0:T(8,128)} %pad_maximum_fusion.2), channel_id=1, source_target_pairs={{0,4},{4,8},{8,12},{12,0},{16,20},{20,24},{24,28},{28,16},{32,36},... | collective-permute-start | bytes 123848 | tf_op jit(solution)/shard_map/ppermute | solution.py:21
  77.5 0.2 fusion.18
  78.2 38.9 %all-gather.2 = f32[64,3,645]{2,1,0:T(4,128)S(1)} all-gather(f32[1,3,645]{2,1,0:T(4,128)S(1)} %maximum_bitcast_fusion.1), channel_id=2, replica_groups=mesh['dp'=2,'ctx'=64,'head'=4] {'ctx'}, dimensions={0}, use_global_device_ids=true | all-gather | bytes 503100 | tf_op jit(solution)/shard_map/all_gather | solution.py:179
  117.2 1.0 reshape.365
  118.2 0.8 slice_bitcast_fusion.3
  119.1 1.0 slice.110
  120.1 0.2 copy.338
  120.3 0.9 convolution_bitcast_fusion.9
  121.2 0.3 fusion.16
  121.5 0.2 convolution_bitcast_fusion.10
  121.7 0.4 convolution_bitcast_fusion.8
  122.1 0.4 fusion.17
  122.5 0.2 slice_reduce_fusion
  122.7 0.7 copy-done.4
  123.4 0.2 copy.319
  123.5 0.8 copy.357
  124.4 0.2 bitcast_select_fusion
  124.5 28.0 %psum.7 = f32[640]{0:T(1024)} all-reduce(f32[640]{0:T(1024)S(1)} %slice_reduce_fusion), channel_id=1, replica_groups=mesh['dp'=2,'ctx'=64,'head'=4] {'dp'}, use_global_device_ids=true, to_apply=%region_23.24 | all-reduce | flops 640 | bytes 5120 | tf_op jit(solution)/shard_map/psum | solution.py:183
  152.5 0.9 pad_maximum_fusion.1
  153.4 0.9 convolution_bitcast_fusion.5
  154.2 0.8 maximum_bitcast_fusion
  155.2 0.2 multiply_convert_fusion.2
  155.5 0.2 convolution_bitcast_fusion.7
  155.7 0.3 fusion.14
  156.0 0.2 copy.350
  156.1 0.8 copy.359
  157.0 0.3 fusion.13
  157.2 0.2 copy.345
  157.4 0.8 copy.358
  158.2 0.3 fusion.15
  158.5 0.2 copy.356
  158.7 0.8 copy.360
  (82 shorter events, 3.9 us)
Async XLA Ops:
  1.5 11.9 %copy-start = (bf16[1,128,640]{2,1,0:T(8,128)(2,1)S(1)}, bf16[1,128,640]{2,1,0:T(8,128)(2,1)}, u32[]{:S(2)}) copy-start(bf16[1,128,640]{2,1,0:T(8,128)(2,1)} %param.6) | copy-start | bytes 491524
  3.0 60.7 %collective-permute-start.2 = (bf16[16,1920]{1,0:T(8,128)(2,1)S(1)}, bf16[16,1920]{1,0:T(8,128)(2,1)S(1)}, u32[]{:S(2)}, u32[]{:S(2)}) collective-permute-start(bf16[16,1920]{1,0:T(8,128)(2,1)S(1)} %bitcast_dynamic-update-slice_fusion), channel_id=1, source_target_pairs={{0,12},{4,0},{8,4},{12,8},{16,28},{20,16},{24,20},{28,24},{32,44},... | collective-permute-start | bytes 184328 | tf_op jit(solution)/shard_map/ppermute | solution.py:21
  9.1 54.7 %collective-permute-start.1 = (bf16[16,1920]{1,0:T(8,128)(2,1)S(1)}, bf16[16,1920]{1,0:T(8,128)(2,1)S(1)}, u32[]{:S(2)}, u32[]{:S(2)}) collective-permute-start(bf16[16,1920]{1,0:T(8,128)(2,1)S(1)} %bitcast_dynamic-update-slice_fusion), channel_id=1, source_target_pairs={{0,8},{4,12},{8,0},{12,4},{16,24},{20,28},{24,16},{28,20},{32,40},... | collective-permute-start | bytes 184328 | tf_op jit(solution)/shard_map/ppermute | solution.py:21
  11.0 52.7 %collective-permute-start = (bf16[16,1920]{1,0:T(8,128)(2,1)S(1)}, bf16[16,1920]{1,0:T(8,128)(2,1)S(1)}, u32[]{:S(2)}, u32[]{:S(2)}) collective-permute-start(bf16[16,1920]{1,0:T(8,128)(2,1)S(1)} %bitcast_dynamic-update-slice_fusion), channel_id=1, source_target_pairs={{0,4},{4,8},{8,12},{12,0},{16,20},{20,24},{24,28},{28,16},{32,36},... | collective-permute-start | bytes 184328 | tf_op jit(solution)/shard_map/ppermute | solution.py:21
  13.4 0.9 copy-start.1
  14.3 0.9 copy-start.2
  15.8 0.9 copy-start.8
  62.7 0.7 copy-start.3
  63.8 0.6 copy-start.6
  64.1 0.6 copy-start.5
  65.8 0.7 copy-start.9
  68.9 83.7 %collective-permute-start.5 = (f32[16,645]{1,0:T(8,128)}, f32[16,645]{1,0:T(8,128)}, u32[]{:S(2)}, u32[]{:S(2)}) collective-permute-start(f32[16,645]{1,0:T(8,128)} %pad_maximum_fusion.2), channel_id=1, source_target_pairs={{0,12},{4,0},{8,4},{12,8},{16,28},{20,16},{24,20},{28,24},{32,44},... | collective-permute-start | bytes 123848 | tf_op jit(solution)/shard_map/ppermute | solution.py:21
  72.8 79.7 %collective-permute-start.4 = (f32[16,645]{1,0:T(8,128)}, f32[16,645]{1,0:T(8,128)}, u32[]{:S(2)}, u32[]{:S(2)}) collective-permute-start(f32[16,645]{1,0:T(8,128)} %pad_maximum_fusion.2), channel_id=1, source_target_pairs={{0,8},{4,12},{8,0},{12,4},{16,24},{20,28},{24,16},{28,20},{32,40},... | collective-permute-start | bytes 123848 | tf_op jit(solution)/shard_map/ppermute | solution.py:21
  75.6 76.9 %collective-permute-start.3 = (f32[16,645]{1,0:T(8,128)}, f32[16,645]{1,0:T(8,128)}, u32[]{:S(2)}, u32[]{:S(2)}) collective-permute-start(f32[16,645]{1,0:T(8,128)} %pad_maximum_fusion.2), channel_id=1, source_target_pairs={{0,4},{4,8},{8,12},{12,0},{16,20},{20,24},{24,28},{28,16},{32,36},... | collective-permute-start | bytes 123848 | tf_op jit(solution)/shard_map/ppermute | solution.py:21
  122.4 0.9 copy-start.4
  154.2 1.0 copy-start.7
where the time goes:
time: 160 us
  blocking collectives  111 us (69%)
  starting transfers between devices  19 us (12%)
  local copies, waits for them, and re-layouts  15.2 us (10%)
  other arithmetic  7.09 us (4%)
  matrix products  6.04 us (4%)
    all_gather x1, blocking collectives, shards(): top_all = lax.all_gather(top_pack, 'ctx', axis=0, tiled=True)  44.2 us
    all_gather x1, blocking collectives, shards(): lax.all_gather(jnp.concatenate([top_grads, gain_row], 0), 'ctx', axis=0)  38.9 us
    psum x1, blocking collectives, shards(): lax.psum(jnp.sum(gathered[:, top_rows, :flat_width], axis=0), 'dp')  28 us
    ppermute x6, starting transfers between devices, group_gather(): pieces.append(lax.ppermute(block, axis, route))  19 us
    unnamed x34, local copies, waits for them, and re-layouts  7.85 us
  transfers between devices with their start and end apart: 6, of which 0 were waited for; matrix products, arithmetic and copies ran while one was open for 7% of the time, Pallas kernels for 0%

commit v1 on v0

--- a/solution.py
+++ b/solution.py
@@ -1,3 +1,4 @@
+import functools
 import math
 import jax
 import jax.numpy as jnp
@@ -8,6 +9,16 @@
 SPAN = 4
 R1 = 8
 EPS = 1e-06
+
+
+def get_bars(content, shard_axis):
+    all_rows = []
+    for _ in range(lax.axis_size(shard_axis)):
+        all_rows.append(content)
+    return jnp.concatenate(lax.all_to_all(jnp.stack(all_rows, axis=0), shard_axis, 0, 0), axis=0)
+
+
+reach_map_in = functools.partial(get_bars, shard_axis="ctx")
 
 
 def group_gather(block, axis, group):
@@ -122,7 +133,7 @@
     mid_rows = mid_pack.shape[0]
     top_rows = top_pack.shape[0]
     mid_all = group_gather(mid_pack, "ctx", SPAN)
-    top_all = lax.all_gather(top_pack, "ctx", axis=0, tiled=True)
+    top_all = reach_map_in(top_pack)
     mid_q, mid_k, mid_v = split_qkv(mid_all, head_count)
     top_q, top_k, top_v = split_qkv(top_all, head_count)
     top_start = my_place * top_rows

time: 160 us -> 135 us (0.84)
  blocking collectives: 111 us -> 55.8 us
  starting transfers between devices: 19 us -> 34.9 us
  waiting for transfers between devices: 0.02 us -> 11.6 us
  local copies, waits for them, and re-layouts: 15.2 us -> 17.4 us
    all_gather x1 -> x0, blocking collectives: 44.2 us -> none  [shards(): top_all = lax.all_gather(top_pack, 'ctx', axis=0, tiled=True)]
    all_to_all x0 -> x1, starting transfers between devices: none -> 14.6 us  [get_bars(): lax.all_to_all(jnp.stack(all_rows, axis=0), shard_axis, 0, 0)]
    all_to_all x0 -> x1, waiting for transfers between devices: none -> 11.6 us  [get_bars(): lax.all_to_all(jnp.stack(all_rows, axis=0), shard_axis, 0, 0)]
    psum x1, blocking collectives: 28 us -> 18.7 us  [shards(): lax.psum(jnp.sum(gathered[:, top_rows, :flat_width], axis=0), 'dp')]
    all_gather x1, blocking collectives: 38.9 us -> 37.1 us  [shards(): lax.all_gather(jnp.concatenate([top_grads, gain_row], 0), 'ctx', axis=0)]
    unnamed x34 -> x49, local copies, waits for them, and re-layouts: 7.85 us -> 8.77 us
  transfers between devices with their start and end apart: 6 -> 7, of which waited for: 0 -> 1; matrix products, arithmetic and copies ran while one was open for 7% -> 9% of each run, Pallas kernels for 0% -> 0%
where the time goes in v1:
time: 135 us
  blocking collectives  55.8 us (41%)
  starting transfers between devices  34.9 us (26%)
  local copies, waits for them, and re-layouts  17.4 us (13%)
  waiting for transfers between devices  11.6 us (9%)
  other arithmetic  7.6 us (6%)
  matrix products  6.05 us (4%)
    all_gather x1, blocking collectives, shards(): lax.all_gather(jnp.concatenate([top_grads, gain_row], 0), 'ctx', axis=0)  37.1 us
    ppermute x6, starting transfers between devices, group_gather(): pieces.append(lax.ppermute(block, axis, route))  20.3 us
    psum x1, blocking collectives, shards(): lax.psum(jnp.sum(gathered[:, top_rows, :flat_width], axis=0), 'dp')  18.7 us
    all_to_all x1, starting transfers between devices, get_bars(): lax.all_to_all(jnp.stack(all_rows, axis=0), shard_axis, 0, 0)  14.6 us
    all_to_all x1, waiting for transfers between devices, get_bars(): lax.all_to_all(jnp.stack(all_rows, axis=0), shard_axis, 0, 0)  11.6 us
    unnamed x49, local copies, waits for them, and re-layouts  8.77 us
  transfers between devices with their start and end apart: 7, of which 1 were waited for; matrix products, arithmetic and copies ran while one was open for 9% of the time, Pallas kernels for 0%

profile of v1, /device:TPU:1, one launch (start us, length us, event | category | flops | bytes accessed | tf_op | source)
XLA Modules:
  0.0 134.6 jit_solution(4235532540895969994)
XLA Ops:
  0.6 0.8 slice_bitcast_fusion.5
  1.4 0.5 copy-done.12
  2.0 1.5 %fusion.24 = (bf16[16,5,128]{2,0,1:T(8,128)(2,1)S(1)}, bf16[16,5,128]{2,0,1:T(8,128)(2,1)S(1)}, bf16[16,5,128]{2,0,1:T(8,128)(2,1)S(1)}) fusion(pred[8,5]{0,1:T(8,128)(4,1)S(1)} %iota_compare_fusion.1, bf16[1,128,640]{2,1,0:T(8,128)(2,1)} %param.6, bf16[1,128,640]{2,1,0:T(8,128)(2,1)} %param.7, bf16[1,128,640]{2,1,0:T(8,128)(2,1)} %param.8), kind=kLoop, calls=%fused_computation.70 | loop fusion | flops 460800 | bytes 553000 | tf_op jit(solution)/shard_map/reduce_sum | solution.py:43
  3.6 6.2 %collective-permute-start.2 = (bf16[16,1920]{1,0:T(8,128)(2,1)S(1)}, bf16[16,1920]{1,0:T(8,128)(2,1)S(1)}, u32[]{:S(2)}, u32[]{:S(2)}) collective-permute-start(bf16[16,1920]{1,0:T(8,128)(2,1)S(1)} %bitcast_dynamic-update-slice_fusion), channel_id=1, source_target_pairs={{0,12},{4,0},{8,4},{12,8},{16,28},{20,16},{24,20},{28,24},{32,44},... | collective-permute-start | bytes 184328 | tf_op jit(solution)/shard_map/ppermute | solution.py:32
  9.8 1.9 %collective-permute-start.1 = (bf16[16,1920]{1,0:T(8,128)(2,1)S(1)}, bf16[16,1920]{1,0:T(8,128)(2,1)S(1)}, u32[]{:S(2)}, u32[]{:S(2)}) collective-permute-start(bf16[16,1920]{1,0:T(8,128)(2,1)S(1)} %bitcast_dynamic-update-slice_fusion), channel_id=1, source_target_pairs={{0,8},{4,12},{8,0},{12,4},{16,24},{20,28},{24,16},{28,20},{32,40},... | collective-permute-start | bytes 184328 | tf_op jit(solution)/shard_map/ppermute | solution.py:32
  11.7 2.3 %collective-permute-start = (bf16[16,1920]{1,0:T(8,128)(2,1)S(1)}, bf16[16,1920]{1,0:T(8,128)(2,1)S(1)}, u32[]{:S(2)}, u32[]{:S(2)}) collective-permute-start(bf16[16,1920]{1,0:T(8,128)(2,1)S(1)} %bitcast_dynamic-update-slice_fusion), channel_id=1, source_target_pairs={{0,4},{4,8},{8,12},{12,0},{16,20},{20,24},{24,28},{28,16},{32,36},... | collective-permute-start | bytes 184328 | tf_op jit(solution)/shard_map/ppermute | solution.py:32
  14.1 0.2 reshape_reshape_squeeze.21
  14.3 0.2 reshape_reshape_squeeze.22
  14.5 0.7 copy-done.2
  15.2 0.2 reshape_reshape_squeeze.23
  15.6 0.3 select_reduce_fusion.2
  15.9 1.0 stack.2
  17.0 14.6 %all-to-all-start = ((bf16[64,2,1920]{2,1,0:T(2,128)(2,1)}), bf16[64,2,1920]{2,1,0:T(2,128)(2,1)S(1)}, u32[]{:S(2)}, u32[]{:S(2)}) async-start(bf16[64,2,1920]{2,1,0:T(2,128)(2,1)} %stack.2), calls=%async_computation | async-start | bytes 983040 | tf_op jit(solution)/shard_map/all_to_all | solution.py:18
  31.8 0.2 copy.227
  32.3 0.5 copy-done.8
  33.2 0.3 fusion.69
  33.5 0.5 and_select_fusion
  34.1 0.2 fusion.68
  34.7 0.2 convolution_bitcast_fusion.4
  35.0 0.2 copy-done.5
  35.2 11.6 %all-to-all-done = bf16[64,2,1920]{2,1,0:T(2,128)(2,1)S(1)} async-done(((bf16[64,2,1920]{2,1,0:T(2,128)(2,1)}), bf16[64,2,1920]{2,1,0:T(2,128)(2,1)S(1)}, u32[]{:S(2)}, u32[]{:S(2)}) %all-to-all-start) | async-done | bytes 491552 | tf_op jit(solution)/shard_map/all_to_all | solution.py:18
  46.8 0.2 reshape.361
  47.3 0.2 copy.248
  47.4 0.2 copy.239
  47.6 0.3 fusion.67
  48.3 0.3 copy-done.17
  48.6 0.4 copy-done.13
  49.2 0.3 fusion.70
  49.5 0.2 fusion.20
  49.8 0.5 multiply_reduce_fusion.3
  50.3 0.7 copy-done.9
  51.0 0.8 multiply_reduce_fusion.2
  51.8 0.3 fusion.19
  52.7 0.6 pad_maximum_fusion.2
  53.3 5.3 %collective-permute-start.5 = (f32[16,645]{1,0:T(8,128)}, f32[16,645]{1,0:T(8,128)}, u32[]{:S(2)}, u32[]{:S(2)}) collective-permute-start(f32[16,645]{1,0:T(8,128)} %pad_maximum_fusion.2), channel_id=1, source_target_pairs={{0,12},{4,0},{8,4},{12,8},{16,28},{20,16},{24,20},{28,24},{32,44},... | collective-permute-start | bytes 123848 | tf_op jit(solution)/shard_map/ppermute | solution.py:32
  58.6 1.9 %collective-permute-start.4 = (f32[16,645]{1,0:T(8,128)}, f32[16,645]{1,0:T(8,128)}, u32[]{:S(2)}, u32[]{:S(2)}) collective-permute-start(f32[16,645]{1,0:T(8,128)} %pad_maximum_fusion.2), channel_id=1, source_target_pairs={{0,8},{4,12},{8,0},{12,4},{16,24},{20,28},{24,16},{28,20},{32,40},... | collective-permute-start | bytes 123848 | tf_op jit(solution)/shard_map/ppermute | solution.py:32
  60.5 2.6 %collective-permute-start.3 = (f32[16,645]{1,0:T(8,128)}, f32[16,645]{1,0:T(8,128)}, u32[]{:S(2)}, u32[]{:S(2)}) collective-permute-start(f32[16,645]{1,0:T(8,128)} %pad_maximum_fusion.2), channel_id=1, source_target_pairs={{0,4},{4,8},{8,12},{12,0},{16,20},{20,24},{24,28},{28,16},{32,36},... | collective-permute-start | bytes 123848 | tf_op jit(solution)/shard_map/ppermute | solution.py:32
  63.2 0.2 fusion.18
  63.4 0.4 copy-done.11
  64.2 37.1 %all-gather.1 = f32[64,3,645]{2,1,0:T(4,128)S(1)} all-gather(f32[1,3,645]{2,1,0:T(4,128)S(1)} %maximum_bitcast_fusion.1), channel_id=2, replica_groups=mesh['dp'=2,'ctx'=64,'head'=4] {'ctx'}, dimensions={0}, use_global_device_ids=true | all-gather | bytes 503100 | tf_op jit(solution)/shard_map/all_gather | solution.py:190
  101.5 1.0 reshape.371
  102.5 0.8 slice_bitcast_fusion.3
  103.3 1.0 slice.110
  104.4 0.2 copy.270
  104.6 0.9 convolution_bitcast_fusion.9
  105.5 0.3 fusion.16
  105.8 0.2 convolution_bitcast_fusion.10
  105.9 0.4 convolution_bitcast_fusion.8
  106.3 0.4 fusion.17
  106.7 0.2 slice_reduce_fusion
  106.9 0.7 copy-done.4
  107.8 0.8 copy.289
  108.8 18.7 %psum.7 = f32[640]{0:T(1024)} all-reduce(f32[640]{0:T(1024)S(1)} %slice_reduce_fusion), channel_id=1, replica_groups=mesh['dp'=2,'ctx'=64,'head'=4] {'dp'}, use_global_device_ids=true, to_apply=%region_23.24 | all-reduce | flops 640 | bytes 5120 | tf_op jit(solution)/shard_map/psum | solution.py:194
  127.5 0.9 pad_maximum_fusion.1
  128.4 0.9 convolution_bitcast_fusion.5
  129.3 0.8 maximum_bitcast_fusion
  130.2 0.2 multiply_convert_fusion.2
  130.5 0.2 convolution_bitcast_fusion.7
  130.7 0.3 fusion.14
  131.2 0.8 copy.291
  132.0 0.3 fusion.13
  132.4 0.8 copy.290
  133.3 0.3 fusion.15
  133.7 0.8 copy.292
  (100 shorter events, 4.9 us)
Async XLA Ops:
  1.4 0.5 copy-start.12
  1.4 14.0 %copy-start.14 = (s32[5]{0:T(128)}, s32[5]{0:T(128)S(1)}, u32[]{:S(2)}) copy-start(s32[5]{0:T(128)S(1)} %get-tuple-element.57) | copy-start | bytes 64
  2.0 12.1 %copy-start = (bf16[1,128,640]{2,1,0:T(8,128)(2,1)S(1)}, bf16[1,128,640]{2,1,0:T(8,128)(2,1)}, u32[]{:S(2)}) copy-start(bf16[1,128,640]{2,1,0:T(8,128)(2,1)} %param.6) | copy-start | bytes 491524
  3.6 10.7 %copy-start.1 = (bf16[1,128,640]{2,1,0:T(8,128)(2,1)S(1)}, bf16[1,128,640]{2,1,0:T(8,128)(2,1)}, u32[]{:S(2)}) copy-start(bf16[1,128,640]{2,1,0:T(8,128)(2,1)} %param.7) | copy-start | bytes 491524
  3.6 30.5 %collective-permute-start.2 = (bf16[16,1920]{1,0:T(8,128)(2,1)S(1)}, bf16[16,1920]{1,0:T(8,128)(2,1)S(1)}, u32[]{:S(2)}, u32[]{:S(2)}) collective-permute-start(bf16[16,1920]{1,0:T(8,128)(2,1)S(1)} %bitcast_dynamic-update-slice_fusion), channel_id=1, source_target_pairs={{0,12},{4,0},{8,4},{12,8},{16,28},{20,16},{24,20},{28,24},{32,44},... | collective-permute-start | bytes 184328 | tf_op jit(solution)/shard_map/ppermute | solution.py:32
  9.8 24.3 %collective-permute-start.1 = (bf16[16,1920]{1,0:T(8,128)(2,1)S(1)}, bf16[16,1920]{1,0:T(8,128)(2,1)S(1)}, u32[]{:S(2)}, u32[]{:S(2)}) collective-permute-start(bf16[16,1920]{1,0:T(8,128)(2,1)S(1)} %bitcast_dynamic-update-slice_fusion), channel_id=1, source_target_pairs={{0,8},{4,12},{8,0},{12,4},{16,24},{20,28},{24,16},{28,20},{32,40},... | collective-permute-start | bytes 184328 | tf_op jit(solution)/shard_map/ppermute | solution.py:32
  11.7 22.3 %collective-permute-start = (bf16[16,1920]{1,0:T(8,128)(2,1)S(1)}, bf16[16,1920]{1,0:T(8,128)(2,1)S(1)}, u32[]{:S(2)}, u32[]{:S(2)}) collective-permute-start(bf16[16,1920]{1,0:T(8,128)(2,1)S(1)} %bitcast_dynamic-update-slice_fusion), channel_id=1, source_target_pairs={{0,4},{4,8},{8,12},{12,0},{16,20},{20,24},{24,28},{28,16},{32,36},... | collective-permute-start | bytes 184328 | tf_op jit(solution)/shard_map/ppermute | solution.py:32
  14.3 0.9 copy-start.2
  15.5 16.6 %copy-start.10 = (pred[64,5]{0,1:T(8,128)(4,1)}, pred[64,5]{0,1:T(8,128)(4,1)S(1)}, u32[]{:S(2)}) copy-start(pred[64,5]{0,1:T(8,128)(4,1)S(1)} %iota_compare_fusion) | copy-start | bytes 964
  17.0 29.9 %all-to-all-start = ((bf16[64,2,1920]{2,1,0:T(2,128)(2,1)}), bf16[64,2,1920]{2,1,0:T(2,128)(2,1)S(1)}, u32[]{:S(2)}, u32[]{:S(2)}) async-start(bf16[64,2,1920]{2,1,0:T(2,128)(2,1)} %stack.2), calls=%async_computation | async-start | bytes 983040 | tf_op jit(solution)/shard_map/all_to_all | solution.py:18
  31.9 0.9 copy-start.8
  34.1 0.6 copy-start.6
  34.6 0.6 copy-start.5
  48.0 0.6 copy-start.17
  48.0 1.5 %copy-start.3 = (bf16[5,128,128]{1,2,0:T(8,128)(2,1)}, bf16[5,128,128]{1,2,0:T(8,128)(2,1)S(1)}, u32[]{:S(2)}) copy-start(bf16[5,128,128]{1,2,0:T(8,128)(2,1)S(1)} %fusion.23) | copy-start | bytes 491524
  48.3 0.6 copy-start.13
  48.3 0.7 copy-start.15
  48.3 0.7 copy-start.16
  50.3 0.7 copy-start.9
  53.3 74.2 %collective-permute-start.5 = (f32[16,645]{1,0:T(8,128)}, f32[16,645]{1,0:T(8,128)}, u32[]{:S(2)}, u32[]{:S(2)}) collective-permute-start(f32[16,645]{1,0:T(8,128)} %pad_maximum_fusion.2), channel_id=1, source_target_pairs={{0,12},{4,0},{8,4},{12,8},{16,28},{20,16},{24,20},{28,24},{32,44},... | collective-permute-start | bytes 123848 | tf_op jit(solution)/shard_map/ppermute | solution.py:32
  58.6 68.9 %collective-permute-start.4 = (f32[16,645]{1,0:T(8,128)}, f32[16,645]{1,0:T(8,128)}, u32[]{:S(2)}, u32[]{:S(2)}) collective-permute-start(f32[16,645]{1,0:T(8,128)} %pad_maximum_fusion.2), channel_id=1, source_target_pairs={{0,8},{4,12},{8,0},{12,4},{16,24},{20,28},{24,16},{28,20},{32,40},... | collective-permute-start | bytes 123848 | tf_op jit(solution)/shard_map/ppermute | solution.py:32
  60.5 67.0 %collective-permute-start.3 = (f32[16,645]{1,0:T(8,128)}, f32[16,645]{1,0:T(8,128)}, u32[]{:S(2)}, u32[]{:S(2)}) collective-permute-start(f32[16,645]{1,0:T(8,128)} %pad_maximum_fusion.2), channel_id=1, source_target_pairs={{0,4},{4,8},{8,12},{12,0},{16,20},{20,24},{24,28},{28,16},{32,36},... | collective-permute-start | bytes 123848 | tf_op jit(solution)/shard_map/ppermute | solution.py:32
  63.2 0.7 copy-start.11
  106.7 0.9 copy-start.4
  129.3 1.0 copy-start.7
